TPU v7x, 32 devices: a whole 2x2x4 slice. The times are simulated.
32 devices in a mesh: group: 2 (over x), blk: 8 (over z, y), ulysses: 2 (over core).
Axes of the slice: x: 2, y: 2, z: 4, core: 2. Of those that a mesh axis runs over, the one named last changes fastest.
Arguments:
- query_int: bfloat16 [4096, 8192], P(('group', 'blk', 'ulysses')), parts along dimension 0, may hold values from -127 to 127, as said below
- key_int: bfloat16 [4096, 1024], P(('group', 'blk', 'ulysses')), parts along dimension 0, may hold values from -127 to 127, as said below
- values: bfloat16 [4096, 1024], P(('group', 'blk', 'ulysses')), parts along dimension 0, may hold values from -6 to 6
- query_scale: bfloat16 [32, 64], P(('group', 'blk')), parts along dimension 0, may hold values from 0.001 to 0.02
- key_scale: bfloat16 [32, 8], P('group'), parts along dimension 0, may hold values from 0.002 to 0.04
- verticals: int32 [16, 8], P('group'), parts along dimension 0, may hold values from 0 to 15, as said below
- slashes: int32 [16, 8], P('group'), parts along dimension 0, may hold values from 0 to 8, as said below
Outputs:
- attention: bfloat16 [4096, 8192], P(('group', 'blk', 'ulysses')), parts along dimension 0
There are 2 independent parts, one for each index of `group`. A program takes and returns all parts, laid end to end along the dimension named above; each array names one. Nothing has to cross between parts.
Inputs may be any that keep to these rules, and one draw needn't show every extreme that they name: `query_int`: integer values. `key_int`: integer values. `verticals`: each row holds 8 distinct key blocks, block 0 among them. `slashes`: each row holds 8 distinct offsets, 0 among them.
All inputs are finite; a program needn't handle non-finite values.
Results may differ from a plain program's by a relative error of at most 0.0019.
Values may be sent and summed in bfloat16 or wider, within the bound.
A program may use at most 128 MiB of HBM per device.

v0:
```python
import jax
import jax.numpy as jnp
from jax import lax
from jax.sharding import PartitionSpec as P

DH = 128
BLOCK = 128


FLOOR_SCORE = -1e30


def block_table(verticals, slashes, first_block, block_count):
    blocks = first_block + jnp.arange(block_count, dtype=jnp.int32)
    slash_keys = blocks[:, None, None] - slashes[None, :, :]
    slash_live = slash_keys >= 0
    vert_keys = jnp.broadcast_to(verticals[None, :, :], (block_count,) + verticals.shape)
    clashes = jnp.any(
        (vert_keys[:, :, :, None] == slash_keys[:, :, None, :]) & slash_live[:, :, None, :], axis=3
    )
    vert_live = (vert_keys <= blocks[:, None, None]) & jnp.logical_not(clashes)
    return (
        jnp.concatenate([vert_keys, slash_keys], axis=2),
        jnp.concatenate([vert_live, slash_live], axis=2),
        blocks,
    )


def gather_blocks(buffer, positions, groups):
    shaped = buffer.reshape(buffer.shape[0] // BLOCK, BLOCK, groups, DH)
    heads_at = jnp.arange(groups, dtype=jnp.int32)[None, :, None]
    return shaped[positions, :, heads_at, :]


def attend_group(pieces):
    query_block, query_scales, key_blocks, value_blocks, key_scales, live_slots, diagonal = pieces
    dots = jnp.einsum("tpd,nsd->ptns", query_block, key_blocks, preferred_element_type=jnp.float32)
    scores = dots * query_scales[:, None, None, None] * key_scales[None, None, :, None]
    width = query_block.shape[0]
    causal = jnp.arange(width)[None, :] <= jnp.arange(width)[:, None]
    allowed = live_slots[None, None, :, None] & (
        jnp.logical_not(diagonal)[None, None, :, None] | causal[None, :, None, :]
    )
    masked = jnp.where(allowed, scores, FLOOR_SCORE)
    largest = jnp.max(masked, axis=(2, 3), keepdims=True)
    weights = jnp.where(allowed, jnp.exp(masked - largest), 0.0)
    totals = jnp.sum(weights, axis=(2, 3))
    numer = jnp.einsum(
        "ptns,nsd->tpd",
        weights.astype(jnp.bfloat16),
        value_blocks,
        preferred_element_type=jnp.float32,
    )
    return (numer / jnp.transpose(totals, (1, 0))[:, :, None]).astype(jnp.bfloat16)


def attend_block(pieces):
    query_block, query_scales, key_blocks, value_blocks, key_scales, live_slots, diagonal = pieces
    by_group = lax.map(
        attend_group,
        (
            jnp.transpose(query_block, (1, 0, 2, 3)),
            query_scales,
            key_blocks,
            value_blocks,
            key_scales,
            live_slots,
            diagonal,
        ),
    )
    return jnp.transpose(by_group, (1, 0, 2, 3))


def local(query_int, key_int, values, query_scale, key_scale, verticals, slashes):
    query_here, key_here, value_here = (
        lax.all_to_all(query_int, "ulysses", split_axis=1, concat_axis=0, tiled=True),
        lax.all_to_all(key_int, "ulysses", split_axis=1, concat_axis=0, tiled=True),
        lax.all_to_all(values, "ulysses", split_axis=1, concat_axis=0, tiled=True),
    )
    half_index = lax.axis_index("ulysses")
    span_index = lax.axis_index("blk")
    span_rows = query_here.shape[0]
    block_count = span_rows // BLOCK
    heads_here = query_here.shape[1] // DH
    groups_here = key_here.shape[1] // DH
    per_group = heads_here // groups_here
    first_block = span_index * block_count
    group_ids = half_index * groups_here + jnp.arange(groups_here, dtype=jnp.int32)
    query_scales = lax.dynamic_slice_in_dim(query_scale, half_index * heads_here, heads_here, 1)
    query_scales = query_scales.astype(jnp.float32).reshape(block_count, groups_here, per_group)
    vert_here = lax.dynamic_slice_in_dim(verticals, half_index * groups_here, groups_here, 0)
    slash_here = lax.dynamic_slice_in_dim(slashes, half_index * groups_here, groups_here, 0)
    block_keys, live_slots, blocks = block_table(vert_here, slash_here, first_block, block_count)
    total_blocks = key_scale.shape[0]
    clipped = jnp.clip(block_keys, 0, total_blocks - 1)
    key_scales = key_scale[clipped, group_ids[None, :, None]].astype(jnp.float32)
    key_all, value_all = (
        lax.all_gather(key_here, "blk", axis=0, tiled=True),
        lax.all_gather(value_here, "blk", axis=0, tiled=True),
    )
    key_blocks = gather_blocks(key_all, clipped, groups_here)
    value_blocks = gather_blocks(value_all, clipped, groups_here)
    diagonal = block_keys == blocks[:, None, None]
    query_blocks = query_here.reshape(block_count, BLOCK, groups_here, per_group, DH)
    outputs = lax.map(
        attend_block,
        (query_blocks, query_scales, key_blocks, value_blocks, key_scales, live_slots, diagonal),
    )
    merged = outputs.reshape(span_rows, heads_here * DH)
    return lax.all_to_all(merged, "ulysses", split_axis=0, concat_axis=1, tiled=True)


def solution(mesh):
    in_specs = (
        P(("group", "blk", "ulysses"), None),
        P(("group", "blk", "ulysses"), None),
        P(("group", "blk", "ulysses"), None),
        P(("group", "blk"), None),
        P("group", None),
        P("group", None),
        P("group", None),
    )
    out_specs = P(("group", "blk", "ulysses"), None)
    return jax.shard_map(local, mesh=mesh, in_specs=in_specs, out_specs=out_specs, check_vma=False)
```

profile of v0, /device:TPU:25, one launch (start us, length us, event | category | flops | bytes accessed | tf_op | source)
XLA Modules:
  0.0 238.6 jit_solution(8448017913891180040)
XLA Ops:
  6.5 1.3 copy.58
  7.8 4.3 %all_to_all.73 = bf16[128,2,512]{0,2,1:T(8,128)(2,1)S(1)} all-to-all(bf16[128,2,512]{0,2,1:T(8,128)(2,1)S(1)} %bitcast.156), channel_id=1, replica_groups=mesh['group'=2,'blk'=8,'ulysses'=2] {'ulysses'}, dimensions={1} | all-to-all | bytes 524288 | tf_op jit(solution)/shard_map/all_to_all | solution.py:77
  12.1 0.8 copy.59
  13.0 1.1 copy.62
  14.1 3.9 %all_to_all.74 = bf16[128,2,512]{0,2,1:T(8,128)(2,1)S(1)} all-to-all(bf16[128,2,512]{0,2,1:T(8,128)(2,1)S(1)} %bitcast.157), channel_id=1, replica_groups=mesh['group'=2,'blk'=8,'ulysses'=2] {'ulysses'}, dimensions={1} | all-to-all | bytes 524288 | tf_op jit(solution)/shard_map/all_to_all | solution.py:78
  18.1 0.9 copy.63
  19.0 2.4 %copy.57 = bf16[128,8192]{0,1:T(8,128)(2,1)} copy(bf16[128,8192]{1,0:T(8,128)(2,1)S(1)} %copy-done.1) | data formatting | bytes 4194304 | tf_op args[0]
  21.4 5.4 %all-to-all-start = ((bf16[128,2,4096]{0,2,1:T(8,128)(2,1)}), bf16[128,2,4096]{0,2,1:T(8,128)(2,1)}, u32[]{:S(2)}, u32[]{:S(2)}) async-start(bf16[128,2,4096]{0,2,1:T(8,128)(2,1)} %bitcast.27), calls=%async_computation | async-start | bytes 4194304 | tf_op jit(solution)/shard_map/all_to_all | solution.py:76
  27.2 1.5 gather_fusion.2
  29.0 0.3 and_reduce_fusion
  29.5 31.3 %all-gather.3.cloned.1.call-done = bf16[2048,512]{1,0:T(8,128)(2,1)} async-done(((bf16[256,512]{1,0:T(8,128)(2,1)}), bf16[2048,512]{1,0:T(8,128)(2,1)}) %all-gather.3.cloned.1.call-update) | async-done | bytes 2097168 | tf_op jit(solution)/shard_map/all_gather | solution.py:98
  60.8 4.0 %reshape.141 = bf16[16,128,4,128]{3,2,1,0:T(4,128)(2,1)} reshape(bf16[2048,512]{1,0:T(8,128)(2,1)} %all-gather.3.cloned.1.call-done) | data formatting | bytes 4194304 | tf_op jit(solution)/shard_map/reshape | solution.py:30
  64.8 2.1 copy.61
  66.9 43.7 %all-gather.5.cloned.1.call-done = bf16[2048,512]{1,0:T(8,128)(2,1)} async-done(((bf16[256,512]{1,0:T(8,128)(2,1)}), bf16[2048,512]{1,0:T(8,128)(2,1)}) %all-gather.5.cloned.1.call-update) | async-done | bytes 2097168 | tf_op jit(solution)/shard_map/all_gather | solution.py:99
  110.6 4.0 %reshape.142 = bf16[16,128,4,128]{3,2,1,0:T(4,128)(2,1)} reshape(bf16[2048,512]{1,0:T(8,128)(2,1)} %all-gather.5.cloned.1.call-done) | data formatting | bytes 4194304 | tf_op jit(solution)/shard_map/reshape | solution.py:30
  114.6 3.5 %copy.65 = bf16[16,128,4,128]{3,1,2,0:T(8,128)(2,1)} copy(bf16[16,128,4,128]{3,2,1,0:T(4,128)(2,1)} %reshape.142) | data formatting | bytes 4194304 | tf_op jit(solution)/shard_map/reshape | solution.py:30
  118.0 3.1 %gather_fusion = bf16[128,128,128]{2,1,0:T(8,128)(2,1)} fusion(bf16[16,128,4,128]{3,1,2,0:T(8,128)(2,1)S(1)} %copy.61, s32[128]{0:T(128)S(1)} %reshape.118), kind=kCustom, calls=%fused_computation | custom fusion | bytes 8389632 | tf_op jit(solution)/shard_map/gather | solution.py:32
  121.1 4.7 %gather_fusion.1 = bf16[128,128,128]{2,1,0:T(8,128)(2,1)} fusion(bf16[16,128,4,128]{3,1,2,0:T(8,128)(2,1)} %copy.65, s32[128]{0:T(128)S(1)} %reshape.118), kind=kCustom, calls=%fused_computation.1 | custom fusion | bytes 8389632 | tf_op jit(solution)/shard_map/gather | solution.py:32
  125.8 89.9 %while.21 = (s32[]{:T(128)}, bf16[2,128,4,8,128]{1,4,3,2,0:T(8,128)(2,1)}, bf16[2,128,4,8,128]{1,4,3,2,0:T(8,128)(2,1)}, f32[2,4,8]{2,1,0:T(4,128)S(1)}, bf16[2,...) while((s32[]{:T(128)}, ...), condition=%wide.region_6.7_spmd, body=%wide.region_1.6_spmd.sunk | while | flops 1108097024 | bytes 46721236 | solution.py:105
  125.8 1.7 constant_dynamic-slice_fusion.13
  127.5 2.6 %copy.84 = bf16[1,4,16,128,128]{3,4,2,1,0:T(8,128)(2,1)} copy(bf16[1,4,16,128,128]{4,3,2,1,0:T(8,128)(2,1)S(1)} %constant_dynamic-slice_fusion.13) | data formatting | bytes 4194304 | tf_op jit(solution)/shard_map/while/body/jit(dynamic_index_in_dim)/dynamic_slice | solution.py:105
  130.1 1.3 constant_dynamic-slice_fusion.14
  131.4 1.4 copy.85
  132.8 1.7 dynamic-slice_bitcast_fusion.6
  134.6 35.1 %while.22 = (s32[]{:T(128)}, bf16[4,128,8,128]{1,3,2,0:T(8,128)(2,1)S(1)}, bf16[4,16,128,128]{2,3,1,0:T(8,128)(2,1)}, pred[4,16]{1,0:T(4,128)(4,1)S(1)}, pred[4,...) while((s32[]{:T(128)}, ...), condition=%wide.region_5.5_spmd, body=%wide.region_2.4_spmd.sunk | while | flops 1108097024 | bytes 27845104 | solution.py:59
  134.6 0.2 or_and_fusion.2
  134.9 2.4 %fusion.58 = (f32[8,128]{1,0:T(8,128)S(1)}, f32[16,128,128,8]{2,1,3,0:T(8,128)S(1)}) fusion(f32[16]{0:T(128)S(1)} %fusion.55, f32[8]{0:T(128)S(1)} %fusion.56, pred[128,16,128]{0,2,1:T(8,128)(4,1)S(1)} %or_and_fusion.2, bf16[4,128,8,128]{3,1,2,0:T(8,128)(2,1)} %get-tuple-element.362, s32[]{:T(128)} %get-tuple-element.346, ...), kind=kOutput, calls=%fused_computation.7.clone.1 | convolution fusion | flops 545258496 | bytes 9443328 | tf_op jit(solution)/shard_map/while/body/eval_jaxpr/while/body/eval_jaxpr/tpd,nsd->ptns/dot_general | solution.py:37
  137.3 2.4 %fusion.59 = f32[8,128]{1,0:T(8,128)S(1)} fusion(f32[16,128,128,8]{2,1,3,0:T(8,128)S(1)} %get-tuple-element.334, f32[8,128]{1,0:T(8,128)S(1)} %get-tuple-element.335, f32[16]{0:T(128)S(1)} %fusion.55, f32[8]{0:T(128)S(1)} %fusion.56, pred[128,16,128]{0,2,1:T(8,128)(4,1)S(1)} %or_and_fusion.2), kind=kLoop, calls=%fused_computation.5.clone.1 | loop fusion | flops 12581888 | bytes 8659040 | tf_op jit(solution)/shard_map/while/body/eval_jaxpr/while/body/eval_jaxpr/reduce_sum | solution.py:47
  139.7 3.6 %fusion.60 = bf16[4,128,8,128]{1,3,2,0:T(8,128)(2,1)S(1)} fusion(bf16[4,128,8,128]{1,3,2,0:T(8,128)(2,1)S(1)} %get-tuple-element.347, s32[]{:T(128)} %get-tuple-element.346, f32[16,128,128,8]{2,1,3,0:T(8,128)S(1)} %get-tuple-element.334, f32[8,128]{1,0:T(8,128)S(1)} %get-tuple-element.335, f32[16]{0:T(128)S(1)} %fusion.55, f32[8]{0:T(128)S(1)} %fusion.56, ...), kind=kOutput, calls=%fused_computation.14.clone.1 | convolution fusion | flops 549715968 | bytes 9447424 | tf_op jit(solution)/shard_map/while/body/eval_jaxpr/while/body/eval_jaxpr/ptns,nsd->tpd/dot_general | solution.py:48
  143.4 0.2 or_and_fusion.2
  143.7 2.4 %fusion.58 = (f32[8,128]{1,0:T(8,128)S(1)}, f32[16,128,128,8]{2,1,3,0:T(8,128)S(1)}) fusion(f32[16]{0:T(128)S(1)} %fusion.55, f32[8]{0:T(128)S(1)} %fusion.56, pred[128,16,128]{0,2,1:T(8,128)(4,1)S(1)} %or_and_fusion.2, bf16[4,128,8,128]{3,1,2,0:T(8,128)(2,1)} %get-tuple-element.362, s32[]{:T(128)} %get-tuple-element.346, ...), kind=kOutput, calls=%fused_computation.7.clone.1 | convolution fusion | flops 545258496 | bytes 9443328 | tf_op jit(solution)/shard_map/while/body/eval_jaxpr/while/body/eval_jaxpr/tpd,nsd->ptns/dot_general | solution.py:37
  146.1 2.4 %fusion.59 = f32[8,128]{1,0:T(8,128)S(1)} fusion(f32[16,128,128,8]{2,1,3,0:T(8,128)S(1)} %get-tuple-element.334, f32[8,128]{1,0:T(8,128)S(1)} %get-tuple-element.335, f32[16]{0:T(128)S(1)} %fusion.55, f32[8]{0:T(128)S(1)} %fusion.56, pred[128,16,128]{0,2,1:T(8,128)(4,1)S(1)} %or_and_fusion.2), kind=kLoop, calls=%fused_computation.5.clone.1 | loop fusion | flops 12581888 | bytes 8659040 | tf_op jit(solution)/shard_map/while/body/eval_jaxpr/while/body/eval_jaxpr/reduce_sum | solution.py:47
  148.5 3.6 %fusion.60 = bf16[4,128,8,128]{1,3,2,0:T(8,128)(2,1)S(1)} fusion(bf16[4,128,8,128]{1,3,2,0:T(8,128)(2,1)S(1)} %get-tuple-element.347, s32[]{:T(128)} %get-tuple-element.346, f32[16,128,128,8]{2,1,3,0:T(8,128)S(1)} %get-tuple-element.334, f32[8,128]{1,0:T(8,128)S(1)} %get-tuple-element.335, f32[16]{0:T(128)S(1)} %fusion.55, f32[8]{0:T(128)S(1)} %fusion.56, ...), kind=kOutput, calls=%fused_computation.14.clone.1 | convolution fusion | flops 549715968 | bytes 9447424 | tf_op jit(solution)/shard_map/while/body/eval_jaxpr/while/body/eval_jaxpr/ptns,nsd->tpd/dot_general | solution.py:48
  152.2 0.2 or_and_fusion.2
  152.5 2.4 %fusion.58 = (f32[8,128]{1,0:T(8,128)S(1)}, f32[16,128,128,8]{2,1,3,0:T(8,128)S(1)}) fusion(f32[16]{0:T(128)S(1)} %fusion.55, f32[8]{0:T(128)S(1)} %fusion.56, pred[128,16,128]{0,2,1:T(8,128)(4,1)S(1)} %or_and_fusion.2, bf16[4,128,8,128]{3,1,2,0:T(8,128)(2,1)} %get-tuple-element.362, s32[]{:T(128)} %get-tuple-element.346, ...), kind=kOutput, calls=%fused_computation.7.clone.1 | convolution fusion | flops 545258496 | bytes 9443328 | tf_op jit(solution)/shard_map/while/body/eval_jaxpr/while/body/eval_jaxpr/tpd,nsd->ptns/dot_general | solution.py:37
  154.9 2.4 %fusion.59 = f32[8,128]{1,0:T(8,128)S(1)} fusion(f32[16,128,128,8]{2,1,3,0:T(8,128)S(1)} %get-tuple-element.334, f32[8,128]{1,0:T(8,128)S(1)} %get-tuple-element.335, f32[16]{0:T(128)S(1)} %fusion.55, f32[8]{0:T(128)S(1)} %fusion.56, pred[128,16,128]{0,2,1:T(8,128)(4,1)S(1)} %or_and_fusion.2), kind=kLoop, calls=%fused_computation.5.clone.1 | loop fusion | flops 12581888 | bytes 8659040 | tf_op jit(solution)/shard_map/while/body/eval_jaxpr/while/body/eval_jaxpr/reduce_sum | solution.py:47
  157.3 3.6 %fusion.60 = bf16[4,128,8,128]{1,3,2,0:T(8,128)(2,1)S(1)} fusion(bf16[4,128,8,128]{1,3,2,0:T(8,128)(2,1)S(1)} %get-tuple-element.347, s32[]{:T(128)} %get-tuple-element.346, f32[16,128,128,8]{2,1,3,0:T(8,128)S(1)} %get-tuple-element.334, f32[8,128]{1,0:T(8,128)S(1)} %get-tuple-element.335, f32[16]{0:T(128)S(1)} %fusion.55, f32[8]{0:T(128)S(1)} %fusion.56, ...), kind=kOutput, calls=%fused_computation.14.clone.1 | convolution fusion | flops 549715968 | bytes 9447424 | tf_op jit(solution)/shard_map/while/body/eval_jaxpr/while/body/eval_jaxpr/ptns,nsd->tpd/dot_general | solution.py:48
  161.2 2.4 %fusion.58 = (f32[8,128]{1,0:T(8,128)S(1)}, f32[16,128,128,8]{2,1,3,0:T(8,128)S(1)}) fusion(f32[16]{0:T(128)S(1)} %fusion.55, f32[8]{0:T(128)S(1)} %fusion.56, pred[128,16,128]{0,2,1:T(8,128)(4,1)S(1)} %or_and_fusion.2, bf16[4,128,8,128]{3,1,2,0:T(8,128)(2,1)} %get-tuple-element.362, s32[]{:T(128)} %get-tuple-element.346, ...), kind=kOutput, calls=%fused_computation.7.clone.1 | convolution fusion | flops 545258496 | bytes 9443328 | tf_op jit(solution)/shard_map/while/body/eval_jaxpr/while/body/eval_jaxpr/tpd,nsd->ptns/dot_general | solution.py:37
  163.6 2.4 %fusion.59 = f32[8,128]{1,0:T(8,128)S(1)} fusion(f32[16,128,128,8]{2,1,3,0:T(8,128)S(1)} %get-tuple-element.334, f32[8,128]{1,0:T(8,128)S(1)} %get-tuple-element.335, f32[16]{0:T(128)S(1)} %fusion.55, f32[8]{0:T(128)S(1)} %fusion.56, pred[128,16,128]{0,2,1:T(8,128)(4,1)S(1)} %or_and_fusion.2), kind=kLoop, calls=%fused_computation.5.clone.1 | loop fusion | flops 12581888 | bytes 8659040 | tf_op jit(solution)/shard_map/while/body/eval_jaxpr/while/body/eval_jaxpr/reduce_sum | solution.py:47
  166.1 3.6 %fusion.60 = bf16[4,128,8,128]{1,3,2,0:T(8,128)(2,1)S(1)} fusion(bf16[4,128,8,128]{1,3,2,0:T(8,128)(2,1)S(1)} %get-tuple-element.347, s32[]{:T(128)} %get-tuple-element.346, f32[16,128,128,8]{2,1,3,0:T(8,128)S(1)} %get-tuple-element.334, f32[8,128]{1,0:T(8,128)S(1)} %get-tuple-element.335, f32[16]{0:T(128)S(1)} %fusion.55, f32[8]{0:T(128)S(1)} %fusion.56, ...), kind=kOutput, calls=%fused_computation.14.clone.1 | convolution fusion | flops 549715968 | bytes 9447424 | tf_op jit(solution)/shard_map/while/body/eval_jaxpr/while/body/eval_jaxpr/ptns,nsd->tpd/dot_general | solution.py:48
  169.7 1.0 bitcast_dynamic-update-slice_fusion.2
  170.7 1.7 constant_dynamic-slice_fusion.13
  172.5 2.6 %copy.84 = bf16[1,4,16,128,128]{3,4,2,1,0:T(8,128)(2,1)} copy(bf16[1,4,16,128,128]{4,3,2,1,0:T(8,128)(2,1)S(1)} %constant_dynamic-slice_fusion.13) | data formatting | bytes 4194304 | tf_op jit(solution)/shard_map/while/body/jit(dynamic_index_in_dim)/dynamic_slice | solution.py:105
  175.1 1.3 constant_dynamic-slice_fusion.14
  176.4 1.4 copy.85
  177.7 1.7 dynamic-slice_bitcast_fusion.6
  179.5 35.1 %while.22 = (s32[]{:T(128)}, bf16[4,128,8,128]{1,3,2,0:T(8,128)(2,1)S(1)}, bf16[4,16,128,128]{2,3,1,0:T(8,128)(2,1)}, pred[4,16]{1,0:T(4,128)(4,1)S(1)}, pred[4,...) while((s32[]{:T(128)}, ...), condition=%wide.region_5.5_spmd, body=%wide.region_2.4_spmd.sunk | while | flops 1108097024 | bytes 27845104 | solution.py:59
  179.8 2.4 %fusion.58 = (f32[8,128]{1,0:T(8,128)S(1)}, f32[16,128,128,8]{2,1,3,0:T(8,128)S(1)}) fusion(f32[16]{0:T(128)S(1)} %fusion.55, f32[8]{0:T(128)S(1)} %fusion.56, pred[128,16,128]{0,2,1:T(8,128)(4,1)S(1)} %or_and_fusion.2, bf16[4,128,8,128]{3,1,2,0:T(8,128)(2,1)} %get-tuple-element.362, s32[]{:T(128)} %get-tuple-element.346, ...), kind=kOutput, calls=%fused_computation.7.clone.1 | convolution fusion | flops 545258496 | bytes 9443328 | tf_op jit(solution)/shard_map/while/body/eval_jaxpr/while/body/eval_jaxpr/tpd,nsd->ptns/dot_general | solution.py:37
  182.3 2.4 %fusion.59 = f32[8,128]{1,0:T(8,128)S(1)} fusion(f32[16,128,128,8]{2,1,3,0:T(8,128)S(1)} %get-tuple-element.334, f32[8,128]{1,0:T(8,128)S(1)} %get-tuple-element.335, f32[16]{0:T(128)S(1)} %fusion.55, f32[8]{0:T(128)S(1)} %fusion.56, pred[128,16,128]{0,2,1:T(8,128)(4,1)S(1)} %or_and_fusion.2), kind=kLoop, calls=%fused_computation.5.clone.1 | loop fusion | flops 12581888 | bytes 8659040 | tf_op jit(solution)/shard_map/while/body/eval_jaxpr/while/body/eval_jaxpr/reduce_sum | solution.py:47
  184.7 3.6 %fusion.60 = bf16[4,128,8,128]{1,3,2,0:T(8,128)(2,1)S(1)} fusion(bf16[4,128,8,128]{1,3,2,0:T(8,128)(2,1)S(1)} %get-tuple-element.347, s32[]{:T(128)} %get-tuple-element.346, f32[16,128,128,8]{2,1,3,0:T(8,128)S(1)} %get-tuple-element.334, f32[8,128]{1,0:T(8,128)S(1)} %get-tuple-element.335, f32[16]{0:T(128)S(1)} %fusion.55, f32[8]{0:T(128)S(1)} %fusion.56, ...), kind=kOutput, calls=%fused_computation.14.clone.1 | convolution fusion | flops 549715968 | bytes 9447424 | tf_op jit(solution)/shard_map/while/body/eval_jaxpr/while/body/eval_jaxpr/ptns,nsd->tpd/dot_general | solution.py:48
  188.6 2.4 %fusion.58 = (f32[8,128]{1,0:T(8,128)S(1)}, f32[16,128,128,8]{2,1,3,0:T(8,128)S(1)}) fusion(f32[16]{0:T(128)S(1)} %fusion.55, f32[8]{0:T(128)S(1)} %fusion.56, pred[128,16,128]{0,2,1:T(8,128)(4,1)S(1)} %or_and_fusion.2, bf16[4,128,8,128]{3,1,2,0:T(8,128)(2,1)} %get-tuple-element.362, s32[]{:T(128)} %get-tuple-element.346, ...), kind=kOutput, calls=%fused_computation.7.clone.1 | convolution fusion | flops 545258496 | bytes 9443328 | tf_op jit(solution)/shard_map/while/body/eval_jaxpr/while/body/eval_jaxpr/tpd,nsd->ptns/dot_general | solution.py:37
  191.0 2.4 %fusion.59 = f32[8,128]{1,0:T(8,128)S(1)} fusion(f32[16,128,128,8]{2,1,3,0:T(8,128)S(1)} %get-tuple-element.334, f32[8,128]{1,0:T(8,128)S(1)} %get-tuple-element.335, f32[16]{0:T(128)S(1)} %fusion.55, f32[8]{0:T(128)S(1)} %fusion.56, pred[128,16,128]{0,2,1:T(8,128)(4,1)S(1)} %or_and_fusion.2), kind=kLoop, calls=%fused_computation.5.clone.1 | loop fusion | flops 12581888 | bytes 8659040 | tf_op jit(solution)/shard_map/while/body/eval_jaxpr/while/body/eval_jaxpr/reduce_sum | solution.py:47
  193.4 3.6 %fusion.60 = bf16[4,128,8,128]{1,3,2,0:T(8,128)(2,1)S(1)} fusion(bf16[4,128,8,128]{1,3,2,0:T(8,128)(2,1)S(1)} %get-tuple-element.347, s32[]{:T(128)} %get-tuple-element.346, f32[16,128,128,8]{2,1,3,0:T(8,128)S(1)} %get-tuple-element.334, f32[8,128]{1,0:T(8,128)S(1)} %get-tuple-element.335, f32[16]{0:T(128)S(1)} %fusion.55, f32[8]{0:T(128)S(1)} %fusion.56, ...), kind=kOutput, calls=%fused_computation.14.clone.1 | convolution fusion | flops 549715968 | bytes 9447424 | tf_op jit(solution)/shard_map/while/body/eval_jaxpr/while/body/eval_jaxpr/ptns,nsd->tpd/dot_general | solution.py:48
  197.4 2.4 %fusion.58 = (f32[8,128]{1,0:T(8,128)S(1)}, f32[16,128,128,8]{2,1,3,0:T(8,128)S(1)}) fusion(f32[16]{0:T(128)S(1)} %fusion.55, f32[8]{0:T(128)S(1)} %fusion.56, pred[128,16,128]{0,2,1:T(8,128)(4,1)S(1)} %or_and_fusion.2, bf16[4,128,8,128]{3,1,2,0:T(8,128)(2,1)} %get-tuple-element.362, s32[]{:T(128)} %get-tuple-element.346, ...), kind=kOutput, calls=%fused_computation.7.clone.1 | convolution fusion | flops 545258496 | bytes 9443328 | tf_op jit(solution)/shard_map/while/body/eval_jaxpr/while/body/eval_jaxpr/tpd,nsd->ptns/dot_general | solution.py:37
  199.8 2.4 %fusion.59 = f32[8,128]{1,0:T(8,128)S(1)} fusion(f32[16,128,128,8]{2,1,3,0:T(8,128)S(1)} %get-tuple-element.334, f32[8,128]{1,0:T(8,128)S(1)} %get-tuple-element.335, f32[16]{0:T(128)S(1)} %fusion.55, f32[8]{0:T(128)S(1)} %fusion.56, pred[128,16,128]{0,2,1:T(8,128)(4,1)S(1)} %or_and_fusion.2), kind=kLoop, calls=%fused_computation.5.clone.1 | loop fusion | flops 12581888 | bytes 8659040 | tf_op jit(solution)/shard_map/while/body/eval_jaxpr/while/body/eval_jaxpr/reduce_sum | solution.py:47
  202.2 3.6 %fusion.60 = bf16[4,128,8,128]{1,3,2,0:T(8,128)(2,1)S(1)} fusion(bf16[4,128,8,128]{1,3,2,0:T(8,128)(2,1)S(1)} %get-tuple-element.347, s32[]{:T(128)} %get-tuple-element.346, f32[16,128,128,8]{2,1,3,0:T(8,128)S(1)} %get-tuple-element.334, f32[8,128]{1,0:T(8,128)S(1)} %get-tuple-element.335, f32[16]{0:T(128)S(1)} %fusion.55, f32[8]{0:T(128)S(1)} %fusion.56, ...), kind=kOutput, calls=%fused_computation.14.clone.1 | convolution fusion | flops 549715968 | bytes 9447424 | tf_op jit(solution)/shard_map/while/body/eval_jaxpr/while/body/eval_jaxpr/ptns,nsd->tpd/dot_general | solution.py:48
  206.2 2.4 %fusion.58 = (f32[8,128]{1,0:T(8,128)S(1)}, f32[16,128,128,8]{2,1,3,0:T(8,128)S(1)}) fusion(f32[16]{0:T(128)S(1)} %fusion.55, f32[8]{0:T(128)S(1)} %fusion.56, pred[128,16,128]{0,2,1:T(8,128)(4,1)S(1)} %or_and_fusion.2, bf16[4,128,8,128]{3,1,2,0:T(8,128)(2,1)} %get-tuple-element.362, s32[]{:T(128)} %get-tuple-element.346, ...), kind=kOutput, calls=%fused_computation.7.clone.1 | convolution fusion | flops 545258496 | bytes 9443328 | tf_op jit(solution)/shard_map/while/body/eval_jaxpr/while/body/eval_jaxpr/tpd,nsd->ptns/dot_general | solution.py:37
  208.6 2.4 %fusion.59 = f32[8,128]{1,0:T(8,128)S(1)} fusion(f32[16,128,128,8]{2,1,3,0:T(8,128)S(1)} %get-tuple-element.334, f32[8,128]{1,0:T(8,128)S(1)} %get-tuple-element.335, f32[16]{0:T(128)S(1)} %fusion.55, f32[8]{0:T(128)S(1)} %fusion.56, pred[128,16,128]{0,2,1:T(8,128)(4,1)S(1)} %or_and_fusion.2), kind=kLoop, calls=%fused_computation.5.clone.1 | loop fusion | flops 12581888 | bytes 8659040 | tf_op jit(solution)/shard_map/while/body/eval_jaxpr/while/body/eval_jaxpr/reduce_sum | solution.py:47
  211.0 3.6 %fusion.60 = bf16[4,128,8,128]{1,3,2,0:T(8,128)(2,1)S(1)} fusion(bf16[4,128,8,128]{1,3,2,0:T(8,128)(2,1)S(1)} %get-tuple-element.347, s32[]{:T(128)} %get-tuple-element.346, f32[16,128,128,8]{2,1,3,0:T(8,128)S(1)} %get-tuple-element.334, f32[8,128]{1,0:T(8,128)S(1)} %get-tuple-element.335, f32[16]{0:T(128)S(1)} %fusion.55, f32[8]{0:T(128)S(1)} %fusion.56, ...), kind=kOutput, calls=%fused_computation.14.clone.1 | convolution fusion | flops 549715968 | bytes 9447424 | tf_op jit(solution)/shard_map/while/body/eval_jaxpr/while/body/eval_jaxpr/ptns,nsd->tpd/dot_general | solution.py:48
  214.6 1.0 bitcast_dynamic-update-slice_fusion.2
  215.7 2.9 %copy.79 = bf16[2,128,4096]{2,1,0:T(8,128)(2,1)S(1)} copy(bf16[2,128,4096]{1,2,0:T(8,128)(2,1)} %bitcast.151) | data formatting | bytes 4194304 | tf_op jit(solution)/shard_map/all_to_all | solution.py:110
  218.6 7.2 %all_to_all.75 = bf16[2,128,4096]{2,1,0:T(8,128)(2,1)} all-to-all(bf16[2,128,4096]{2,1,0:T(8,128)(2,1)S(1)} %copy.79), channel_id=1, replica_groups=mesh['group'=2,'blk'=8,'ulysses'=2] {'ulysses'}, dimensions={0} | all-to-all | bytes 4194304 | tf_op jit(solution)/shard_map/all_to_all | solution.py:110
  225.7 3.1 %copy.69 = bf16[2,128,4096]{1,2,0:T(8,128)(2,1)S(1)} copy(bf16[2,128,4096]{2,1,0:T(8,128)(2,1)} %all_to_all.75) | data formatting | bytes 4194304 | tf_op jit(solution)/shard_map/all_to_all | solution.py:110
  228.9 2.9 %copy.70 = bf16[128,8192]{1,0:T(8,128)(2,1)} copy(bf16[128,8192]{0,1:T(8,128)(2,1)S(1)} %bitcast.149) | data formatting | bytes 4194304 | tf_op jit(solution)/shard_map/all_to_all | solution.py:110
  (77 shorter events, 2.6 us)
Async XLA Ops:
  6.5 20.6 %copy-start = (bf16[16,8]{0,1:T(8,128)(2,1)S(1)}, bf16[16,8]{0,1:T(8,128)(2,1)}, u32[]{:S(2)}) copy-start(bf16[16,8]{0,1:T(8,128)(2,1)} %param.15) | copy-start | bytes 772
  6.5 12.4 %copy-start.1 = (bf16[128,8192]{1,0:T(8,128)(2,1)S(1)}, bf16[128,8192]{1,0:T(8,128)(2,1)}, u32[]{:S(2)}) copy-start(bf16[128,8192]{1,0:T(8,128)(2,1)} %param.11) | copy-start | bytes 6291460
  6.5 54.3 %all-gather.3.cloned.1.call-start = ((), (), s32[]{:S(2)}) async-start(), calls=%async_computation.4 | async-start | bytes 2359296 | tf_op jit(solution)/shard_map/all_gather | solution.py:98
  12.9 97.6 %all-gather.5.cloned.1.call-start = ((), (), s32[]{:S(2)}) async-start(), calls=%async_computation.5 | async-start | bytes 2359296 | tf_op jit(solution)/shard_map/all_gather | solution.py:99
  19.0 7.9 %copy-start.2 = (s32[8,8]{1,0:T(8,128)S(1)}, s32[8,8]{1,0:T(8,128)}, u32[]{:S(2)}) copy-start(s32[8,8]{1,0:T(8,128)} %param.17) | copy-start | bytes 772
  19.0 7.9 %copy-start.3 = (s32[8,8]{1,0:T(8,128)S(1)}, s32[8,8]{1,0:T(8,128)}, u32[]{:S(2)}) copy-start(s32[8,8]{1,0:T(8,128)} %param.16) | copy-start | bytes 772
  21.4 7.4 %copy-start.4 = (bf16[2,64]{1,0:T(2,128)(2,1)S(1)}, bf16[2,64]{1,0:T(2,128)(2,1)}, u32[]{:S(2)}) copy-start(bf16[2,64]{1,0:T(2,128)(2,1)} %param.14) | copy-start | bytes 772
  21.4 104.4 %all-to-all-start = ((bf16[128,2,4096]{0,2,1:T(8,128)(2,1)}), bf16[128,2,4096]{0,2,1:T(8,128)(2,1)}, u32[]{:S(2)}, u32[]{:S(2)}) async-start(bf16[128,2,4096]{0,2,1:T(8,128)(2,1)} %bitcast.27), calls=%async_computation | async-start | bytes 4194304 | tf_op jit(solution)/shard_map/all_to_all | solution.py:76
Sparse Core Ops, SparseCore 0:
  13.1 47.7 all-gather.2
  62.9 47.6 all-gather.4
where the time goes:
time: 243 us; the launch traced here: 239 us
  waiting for transfers between devices  75 us (31%)
  local copies, waits for them, and re-layouts  58.4 us (24%)
  matrix products  48.1 us (20%)
  other arithmetic  22.2 us (9%)
  blocking collectives  15.4 us (6%)
  between operations  13.5 us (6%)
  starting transfers between devices  5.41 us (2%)
    all_gather x1, waiting for transfers between devices, local(): lax.all_gather(value_here, 'blk', axis=0, tiled=True)  43.7 us
    all_gather x1, waiting for transfers between devices, local(): lax.all_gather(key_here, 'blk', axis=0, tiled=True)  31.3 us
    dot_general x8, matrix products, attend_group(): jnp.einsum('ptns,nsd->tpd', weights.astype(jnp.bfloat16), value_blocks, p...  28.8 us
    reduce_sum x8, other arithmetic, attend_group(): totals = jnp.sum(weights, axis=(2, 3))  19.3 us
    dot_general x8, matrix products, attend_group(): jnp.einsum('tpd,nsd->ptns', query_block, key_blocks, preferred_element_ty...  19.2 us
    dynamic_slice x8, local copies, waits for them, and re-layouts, local(): lax.map(attend_block, (query_blocks, query_scales, key_blocks, value_bloc...  14 us
    reshape x4, local copies, waits for them, and re-layouts, gather_blocks(): shaped = buffer.reshape(buffer.shape[0] // BLOCK, BLOCK, groups, DH)  13.5 us
    all_to_all x3, local copies, waits for them, and re-layouts, local(): lax.all_to_all(merged, 'ulysses', split_axis=0, concat_axis=1, tiled=True)  8.94 us
  transfers between devices with their start and end apart: 3, of which 2 were waited for; matrix products, arithmetic and copies ran while one was open for 12% of the time, Pallas kernels for 0%

commit v1 on v0

v1 whole, which is shorter than its diff:
```python
import functools
import math

import jax
import jax.numpy as jnp
from jax import lax
from jax.experimental import pallas as pl
from jax.experimental.pallas import tpu as pltpu
from jax.sharding import PartitionSpec as P

BLOCK = 128
DH = 128
BIG = 2.0**40
LOG2E = math.log2(math.e)
MESH = pl.DeviceIdType.MESH
UP, ACROSS, CHIP = 0, 1, 2


def kernel(
    rows, heads, groups, q_hbm, k_hbm, v_hbm, qs_ref, ks_ref, bias_ref, o_hbm,
    q_ref, kv_ref, m_ref, l_ref, acc_ref, o_ref, local_sem, out_sem, send_sem, recv_sem,
):
    span = lax.axis_index("blk")
    core = lax.axis_index("ulysses")
    row, col = span // 2, span % 2
    mine = span * 2 + core
    per_group = heads // groups
    width = per_group * DH
    sources = (k_hbm, v_hbm)

    def block_of(r, c, u):
        return (r * 2 + c) * 2 + u

    def target(way):
        if way == UP:
            return {"blk": span + 2, "ulysses": core}
        if way == ACROSS:
            return {"blk": row * 2 + 1 - col, "ulysses": core}
        return {"blk": span, "ulysses": 1 - core}

    def remote(which, block, way, own=False):
        place = kv_ref.at[which, block]
        return pltpu.make_async_remote_copy(
            src_ref=sources[which] if own else place,
            dst_ref=place,
            send_sem=send_sem.at[which, way, block],
            recv_sem=recv_sem.at[which, block],
            device_id=target(way),
            device_id_type=MESH,
        )

    def arrived(which, block):
        remote(which, block, CHIP).wait_recv()

    def local_copy(which):
        return pltpu.make_async_copy(sources[which], kv_ref.at[which, mine], local_sem.at[which])

    q_copy = pltpu.make_async_copy(q_hbm, q_ref, local_sem.at[2])
    q_copy.start()
    local_copy(0).start()
    local_copy(1).start()

    barrier = pltpu.get_barrier_semaphore()
    below, above = row > 0, row < rows - 1

    @pl.when(above)
    def _():
        pl.semaphore_signal(
            barrier, inc=1, device_id={"blk": span + 2, "ulysses": core}, device_id_type=MESH
        )

    @pl.when(below)
    def _():
        pl.semaphore_signal(
            barrier, inc=1, device_id={"blk": span - 2, "ulysses": core}, device_id_type=MESH
        )

    for way in (ACROSS, CHIP):
        pl.semaphore_signal(barrier, inc=1, device_id=target(way), device_id_type=MESH)
    pl.semaphore_wait(barrier, 2 + below.astype(jnp.int32) + above.astype(jnp.int32))

    def send_on(which, block, own=False):
        @pl.when(above)
        def _():
            remote(which, block, UP, own).start()

        remote(which, block, ACROSS, own).start()
        remote(which, block, CHIP, own).start()

    for which in (0, 1):
        send_on(which, mine, own=True)

    token = lax.broadcasted_iota(jnp.int32, (BLOCK, BLOCK), 1)
    key_at = lax.broadcasted_iota(jnp.int32, (BLOCK, BLOCK), 0)
    later = jnp.where(key_at > token, 1.0, 0.0)
    eye = jnp.where(key_at == token, 1.0, 0.0).astype(jnp.bfloat16)

    def hidden(block, g):
        own = jnp.where(block == mine, -BIG, 0.0)
        return (bias_ref[block, g] + later * own).astype(jnp.bfloat16)

    def unit(pairs, g, first, last):
        lanes = pl.ds(pl.multiple_of(g * DH, DH), DH)
        queries = jnp.concatenate(
            [
                jnp.concatenate(
                    [q_ref[:, pl.ds(pl.multiple_of(g * width + p * DH, DH), DH)], eye], axis=1
                )
                for p in range(per_group)
            ],
            axis=0,
        )
        scores, scales = [], []
        for base in pairs:
            keys = kv_ref[0, pl.ds(base, 2), :, lanes].reshape(2 * BLOCK, DH)
            mask = jnp.concatenate([hidden(base, g), hidden(base + 1, g)], axis=0)
            scores.append(
                lax.dot_general(
                    queries,
                    jnp.concatenate([keys, mask], axis=1),
                    (((1,), (1,)), ((), ())),
                    preferred_element_type=jnp.float32,
                )
            )
            scales += [ks_ref[base, g], ks_ref[base + 1, g]]
        probs, alphas = [], []
        for p in range(per_group):
            here = slice(p * BLOCK, (p + 1) * BLOCK)
            q_scale = qs_ref[0, g * per_group + p]
            tiles = [
                scores[i // 2][here, (i % 2) * BLOCK : (i % 2 + 1) * BLOCK] * (q_scale * scales[i])
                for i in range(2 * len(pairs))
            ]
            top = functools.reduce(jnp.maximum, tiles)
            top = jnp.max(top, axis=1, keepdims=True)
            top = jnp.broadcast_to(top, (BLOCK, DH))
            if not first:
                old = m_ref[g, here, :]
                top = jnp.maximum(old, top)
                alpha = jnp.exp2(old - top)
                alphas.append(alpha)
            weights = [jnp.exp2(tile - top) for tile in tiles]
            total = functools.reduce(jnp.add, weights)
            if not first:
                total = l_ref[g, here, :] * alpha + total
            l_ref[g, here, :] = total
            if not last:
                m_ref[g, here, :] = top
            probs.append(jnp.concatenate([w.astype(jnp.bfloat16) for w in weights], axis=1))
        probs = jnp.concatenate(probs, axis=0)
        held = [kv_ref[1, pl.ds(base, 2), :, lanes].reshape(2 * BLOCK, DH) for base in pairs]
        held = held[0] if len(held) == 1 else jnp.concatenate(held, axis=0)
        added = jnp.dot(probs, held, preferred_element_type=jnp.float32)
        for p in range(per_group):
            here = slice(p * BLOCK, (p + 1) * BLOCK)
            numer = added[here, :]
            if not first:
                numer = acc_ref[g, here, :] * alphas[p] + numer
            if last:
                total = jnp.sum(l_ref[g, here, :], axis=1, keepdims=True)
                o_ref[:, pl.ds(pl.multiple_of(g * width + p * DH, DH), DH)] = (
                    numer * (1.0 / total)
                ).astype(o_ref.dtype)
            else:
                acc_ref[g, here, :] = numer

    def out_copy(g):
        part = pl.ds(pl.multiple_of(g * width, DH), width)
        return pltpu.make_async_copy(o_ref.at[:, part], o_hbm.at[:, part], out_sem.at[g])

    q_copy.wait()
    for which in (0, 1):
        local_copy(which).wait()
        arrived(which, block_of(row, col, 1 - core))

    @pl.loop(0, groups)
    def _(g):
        unit([block_of(row, col, 0)], g, True, False)

    @pl.loop(1, row + 1)
    def _(k):
        for which in (0, 1):
            climbed = block_of(row - k, col, core)
            arrived(which, climbed)
            send_on(which, climbed)
            crossed = block_of(row - k + 1, 1 - col, core)
            arrived(which, crossed)
            remote(which, crossed, CHIP).start()
        for which in (0, 1):
            arrived(which, block_of(row - k, col, 1 - core))
            arrived(which, block_of(row - k + 1, 1 - col, 1 - core))

        @pl.loop(0, groups)
        def _(g):
            unit([block_of(row - k, col, 0), block_of(row - k + 1, 1 - col, 0)], g, False, False)

    for which in (0, 1):
        crossed = block_of(0, 1 - col, core)
        arrived(which, crossed)
        remote(which, crossed, CHIP).start()
    for which in (0, 1):
        arrived(which, block_of(0, 1 - col, 1 - core))

    @pl.loop(0, groups)
    def _(g):
        unit([block_of(0, 1 - col, 0)], g, False, True)
        out_copy(g).start()

    @pl.loop(0, row + 1)
    def _(k):
        for which in (0, 1):
            climbed = block_of(row - k, col, core)

            @pl.when(above)
            def _():
                remote(which, climbed, UP).wait_send()

            remote(which, climbed, ACROSS).wait_send()
            remote(which, climbed, CHIP).wait_send()
            remote(which, block_of(row - k, 1 - col, core), CHIP).wait_send()

    @pl.loop(0, groups)
    def _(g):
        out_copy(g).wait()


def attend(mesh, query_int, key_int, values, query_scale, key_scale, verticals, slashes):
    spans = mesh.shape["blk"]
    tokens = query_int.shape[0]
    blocks = key_scale.shape[0]
    heads = query_int.shape[1] // DH
    groups = key_int.shape[1] // DH
    assert tokens == BLOCK and mesh.shape["ulysses"] == 2 and spans % 2 == 0
    assert blocks == spans * 2
    core = lax.axis_index("ulysses")
    mine = lax.axis_index("blk") * 2 + core
    block = jnp.arange(blocks, dtype=jnp.int32)[:, None, None]
    live = jnp.any(block == mine - slashes[None], axis=2) | (
        jnp.any(block == verticals[None], axis=2) & (block[:, :, 0] <= mine)
    )
    bias = jnp.where(live, 0.0, -BIG).astype(jnp.float32)
    key_scales = key_scale.astype(jnp.float32) * LOG2E
    query_scales = lax.dynamic_slice_in_dim(query_scale, core, 1, 0).astype(jnp.float32)
    per_group = heads // groups
    stack = (groups, per_group * BLOCK, DH)
    smem = pl.BlockSpec(memory_space=pltpu.SMEM)
    hbm = pl.BlockSpec(memory_space=pl.ANY)
    return pl.pallas_call(
        functools.partial(kernel, spans // 2, heads, groups),
        out_shape=jax.ShapeDtypeStruct(query_int.shape, jnp.bfloat16),
        in_specs=[hbm, hbm, hbm, smem, smem, smem],
        out_specs=hbm,
        scratch_shapes=[
            pltpu.VMEM(query_int.shape, jnp.bfloat16),
            pltpu.VMEM((2, blocks) + key_int.shape, jnp.bfloat16),
            pltpu.VMEM(stack, jnp.float32),
            pltpu.VMEM(stack, jnp.float32),
            pltpu.VMEM(stack, jnp.float32),
            pltpu.VMEM(query_int.shape, jnp.bfloat16),
            pltpu.SemaphoreType.DMA((3,)),
            pltpu.SemaphoreType.DMA((groups,)),
            pltpu.SemaphoreType.DMA((2, 3, blocks)),
            pltpu.SemaphoreType.DMA((2, blocks)),
        ],
        compiler_params=pltpu.CompilerParams(
            collective_id=0, has_side_effects=True, vmem_limit_bytes=62 * 1024 * 1024
        ),
    )(query_int, key_int, values, query_scales, key_scales, bias)


def solution(mesh):
    in_specs = (
        P(("group", "blk", "ulysses"), None),
        P(("group", "blk", "ulysses"), None),
        P(("group", "blk", "ulysses"), None),
        P(("group", "blk"), None),
        P("group", None),
        P("group", None),
        P("group", None),
    )
    out_specs = P(("group", "blk", "ulysses"), None)
    return jax.shard_map(
        functools.partial(attend, mesh),
        mesh=mesh,
        in_specs=in_specs,
        out_specs=out_specs,
        check_vma=False,
    )
```

time: 243 us -> 65.6 us (0.27); the launches traced: 239 us -> 65.3 us
  waiting for transfers between devices: 75 us -> 0 us
  Pallas kernels: 0 us -> 57.8 us
  local copies, waits for them, and re-layouts: 58.4 us -> 4.03 us
  matrix products: 48.1 us -> 0 us
  other arithmetic: 22.2 us -> 3.45 us
  blocking collectives: 15.4 us -> 0 us
  between operations: 13.5 us -> 0.01 us
  starting transfers between devices: 5.41 us -> 0 us
    all_gather x2 -> x0, waiting for transfers between devices: 74.9 us -> none  [the longest x1 43.7 us: local(): lax.all_gather(value_here, 'blk', axis=0, tiled=True)]
    pallas_call x0 -> x1, Pallas kernels: none -> 57.8 us  [attend(): pl.pallas_call(functools.partial(kernel, spans // 2, heads, groups), out_...]
    dot_general x16 -> x0, matrix products: 48.1 us -> none  [the longest x8 28.8 us: attend_group(): jnp.einsum('ptns,nsd->tpd', weights.astype(jnp.bfloat16), value_blocks, p...]
    reduce_sum x8 -> x0, other arithmetic: 19.3 us -> none  [attend_group(): totals = jnp.sum(weights, axis=(2, 3))]
    all_to_all x3 -> x0, blocking collectives: 15.4 us -> none  [the longest x1 7.15 us: local(): lax.all_to_all(merged, 'ulysses', split_axis=0, concat_axis=1, tiled=True)]
    dynamic_slice x9 -> x0, local copies, waits for them, and re-layouts: 14 us -> none  [the longest x8 14 us: local(): lax.map(attend_block, (query_blocks, query_scales, key_blocks, value_bloc...]
    reshape x5 -> x0, local copies, waits for them, and re-layouts: 13.6 us -> none  [the longest x4 13.5 us: gather_blocks(): shaped = buffer.reshape(buffer.shape[0] // BLOCK, BLOCK, groups, DH)]
    all_to_all x5 -> x0, local copies, waits for them, and re-layouts: 10.6 us -> none  [the longest x3 8.94 us: local(): lax.all_to_all(merged, 'ulysses', split_axis=0, concat_axis=1, tiled=True)]
  transfers between devices with their start and end apart: 3 -> 0, of which waited for: 2 -> 0; matrix products, arithmetic and copies ran while one was open for 12% -> 0% of each run, Pallas kernels for 0% -> 0%
where the time goes in v1:
time: 65.6 us; the launch traced here: 65.3 us
  Pallas kernels  57.8 us (88%)
  local copies, waits for them, and re-layouts  4.03 us (6%)
  other arithmetic  3.45 us (5%)
    pallas_call x1, Pallas kernels, attend(): pl.pallas_call(functools.partial(kernel, spans // 2, heads, groups), out_...  57.8 us
    unnamed x1, local copies, waits for them, and re-layouts  3.1 us

profile of v1, /device:TPU:25, one launch (start us, length us, event | category | flops | bytes accessed | tf_op | source)
XLA Modules:
  0.0 65.3 jit_solution(14989575105575113250)
XLA Ops:
  0.0 1.2 %dynamic-slice_convert_fusion.qs_ref = f32[1,64]{1,0:T(1,128)} fusion(bf16[2,64]{1,0:T(2,128)(2,1)} %param.10, s32[]{:T(128)S(6)} %select_n.7), kind=kLoop, calls=%fused_computation.8 | loop fusion | flops 64 | bytes 388 | tf_op jit(solution)/shard_map/convert_element_type | solution.py:243
  1.2 0.8 %fusion.1 = pred[16,8]{0,1:T(8,128)(4,1)S(1)} fusion(s32[8,8]{1,0:T(8,128)} %param.12), kind=kLoop, calls=%fused_computation.3 | loop fusion | flops 1920 | bytes 384 | tf_op jit(solution)/shard_map/reduce_or | solution.py:239
  2.0 0.1 copy.13
  2.1 0.7 %broadcast_subtract_fusion = s32[8,8]{1,0:T(8,128)S(1)} fusion(s32[8,8]{1,0:T(8,128)} %param.13, s32[]{:T(128)S(6)} %add.7), kind=kLoop, calls=%fused_computation.6 | loop fusion | flops 64 | bytes 516 | tf_op jit(solution)/shard_map/sub | solution.py:238
  2.8 0.1 fusion
  2.9 0.1 copy.14
  3.0 0.8 %copy.12 = f32[16,8]{1,0:T(8,128)S(1)} copy(bf16[16,8]{0,1:T(8,128)(2,1)} %param.11) | data formatting | bytes 768 | tf_op jit(solution)/shard_map/convert_element_type | solution.py:242
  3.7 0.7 %or_select_fusion = (f32[16,8]{1,0:T(8,128)}, f32[16,8]{1,0:T(8,128)}) fusion(pred[16,8]{1,0:T(8,128)(4,1)S(1)} %copy.14, pred[16,8]{1,0:T(8,128)(4,1)S(1)} %copy.13, pred[16]{0:T(512)(128)(4,1)S(1)} %iota_compare_fusion.2, f32[16,8]{1,0:T(8,128)S(1)} %copy.12), kind=kLoop, calls=%fused_computation.4 | loop fusion | flops 512 | bytes 1808 | tf_op jit(solution)/shard_map/jit(_where)/select_n | solution.py:241
  4.4 57.8 %shard_map.73 = bf16[128,8192]{1,0:T(8,128)(2,1)} custom-call(bf16[128,8192]{1,0:T(8,128)(2,1)} %q_hbm.1, bf16[128,1024]{1,0:T(8,128)(2,1)} %k_hbm.1, bf16[128,1024]{1,0:T(8,128)(2,1)} %v_hbm.1, f32[1,64]{1,0:T(1,128)} %dynamic-slice_convert_fusion.qs_ref, f32[16,8]{1,0:T(8,128)} %get-tuple-element.6.ks_ref, f32[16,8]{1,0:T(8,128)} %get-tuple-element.5.bias_ref), custom_call_target="tpu_custom_call" | custom-call | tf_op jit(solution)/shard_map/pallas_call | solution.py:248
  62.2 3.1 %copy.16 = bf16[128,8192]{1,0:T(8,128)(2,1)} copy(bf16[128,8192]{1,0:T(8,128)(2,1)} %shard_map.73) | data formatting | bytes 4194304
  (1 shorter events, 0.0 us)

commit v2 on v1

v2 whole, which is shorter than its diff:
```python
import functools
import math

import jax
import jax.numpy as jnp
from jax import lax
from jax.experimental import pallas as pl
from jax.experimental.pallas import tpu as pltpu
from jax.sharding import PartitionSpec as P

BLOCK = 128
DH = 128
BIG = 2.0**40
LOG2E = math.log2(math.e)
MESH = pl.DeviceIdType.MESH
UP, ACROSS, CHIP = 0, 1, 2


def kernel(
    rows, heads, groups, blocks, q_hbm, k_hbm, v_hbm, qs_hbm, ks_hbm, vert_hbm, slash_hbm, o_hbm,
    q_ref, kv_ref, m_ref, l_ref, acc_ref, o_ref, qs_ref, ks_ref, vert_ref, slash_ref,
    table_ref, scalar_ref, local_sem, small_sem, out_sem, send_sem, recv_sem,
):
    span = lax.axis_index("blk")
    core = lax.axis_index("ulysses")
    row, col = span // 2, span % 2
    mine = span * 2 + core
    per_group = heads // groups
    width = per_group * DH
    per_half = groups // 2
    half_lanes = per_half * DH

    def block_of(r, c, u):
        return (r * 2 + c) * 2 + u

    def target(way):
        if way == UP:
            return {"blk": span + 2, "ulysses": core}
        if way == ACROSS:
            return {"blk": row * 2 + 1 - col, "ulysses": core}
        return {"blk": span, "ulysses": 1 - core}

    def remote(half, block, way):
        place = kv_ref.at[half, block]
        return pltpu.make_async_remote_copy(
            src_ref=place,
            dst_ref=place,
            send_sem=send_sem.at[half, way, block],
            recv_sem=recv_sem.at[half, block],
            device_id=target(way),
            device_id_type=MESH,
        )

    def arrived(half, block):
        remote(half, block, CHIP).wait_recv()

    def local_copy(half, which):
        return pltpu.make_async_copy(
            (k_hbm, v_hbm)[which].at[:, pl.ds(half * half_lanes, half_lanes)],
            kv_ref.at[half, mine, which],
            local_sem.at[half, which],
        )

    small = [
        pltpu.make_async_copy(src, dst, small_sem.at[i])
        for i, (src, dst) in enumerate(
            [(qs_hbm, qs_ref), (ks_hbm, ks_ref), (vert_hbm, vert_ref), (slash_hbm, slash_ref)]
        )
    ]
    to_scalars = pltpu.make_async_copy(table_ref, scalar_ref, small_sem.at[4])
    q_copy = pltpu.make_async_copy(q_hbm, q_ref, small_sem.at[5])
    for half in (0, 1):
        for which in (0, 1):
            local_copy(half, which).start()
    for copy in small:
        copy.start()
    q_copy.start()

    barrier = pltpu.get_barrier_semaphore()
    below, above = row > 0, row < rows - 1

    @pl.when(above)
    def _():
        pl.semaphore_signal(
            barrier, inc=1, device_id={"blk": span + 2, "ulysses": core}, device_id_type=MESH
        )

    @pl.when(below)
    def _():
        pl.semaphore_signal(
            barrier, inc=1, device_id={"blk": span - 2, "ulysses": core}, device_id_type=MESH
        )

    for way in (ACROSS, CHIP):
        pl.semaphore_signal(barrier, inc=1, device_id=target(way), device_id_type=MESH)
    pl.semaphore_wait(barrier, 2 + below.astype(jnp.int32) + above.astype(jnp.int32))

    for half in (0, 1):
        for which in (0, 1):
            local_copy(half, which).wait()

        @pl.when(above)
        def _():
            remote(half, mine, UP).start()

        remote(half, mine, ACROSS).start()
        remote(half, mine, CHIP).start()

    for copy in small:
        copy.wait()
    key_block = lax.broadcasted_iota(jnp.int32, (groups, 128), 1)
    slashes, verticals = slash_ref[...], vert_ref[...]
    hits = jnp.zeros((groups, 128), jnp.int32)
    for j in range(slashes.shape[1]):
        hits += jnp.where(key_block == mine - slashes[:, j : j + 1], 1, 0)
    for j in range(verticals.shape[1]):
        hits += jnp.where((key_block == verticals[:, j : j + 1]) & (key_block <= mine), 1, 0)
    table_ref[0] = jnp.where(hits > 0, 0.0, -BIG)
    table_ref[1, :, :blocks] = ks_ref[...].astype(jnp.float32) * LOG2E
    query_scales = qs_ref[...].astype(jnp.float32)
    table_ref[2, 0:1, :heads] = jnp.where(core == 0, query_scales[0:1], query_scales[1:2])
    to_scalars.start()

    token = lax.broadcasted_iota(jnp.int32, (BLOCK, BLOCK), 1)
    key_at = lax.broadcasted_iota(jnp.int32, (BLOCK, BLOCK), 0)
    later = jnp.where(key_at > token, 1.0, 0.0)
    eye = jnp.where(key_at == token, 1.0, 0.0).astype(jnp.bfloat16)

    def hidden(block, g):
        own = jnp.where(block == mine, -BIG, 0.0)
        return (scalar_ref[0, g, block] + later * own).astype(jnp.bfloat16)

    def unit(pairs, g, first, last):
        half = g // per_half
        lanes = pl.ds(pl.multiple_of((g - half * per_half) * DH, DH), DH)
        queries = jnp.concatenate(
            [
                jnp.concatenate(
                    [q_ref[:, pl.ds(pl.multiple_of(g * width + p * DH, DH), DH)], eye], axis=1
                )
                for p in range(per_group)
            ],
            axis=0,
        )
        scores, scales = [], []
        for base in pairs:
            keys = kv_ref[half, pl.ds(base, 2), 0, :, lanes].reshape(2 * BLOCK, DH)
            mask = jnp.concatenate([hidden(base, g), hidden(base + 1, g)], axis=0)
            scores.append(
                lax.dot_general(
                    queries,
                    jnp.concatenate([keys, mask], axis=1),
                    (((1,), (1,)), ((), ())),
                    preferred_element_type=jnp.float32,
                )
            )
            scales += [scalar_ref[1, g, base], scalar_ref[1, g, base + 1]]
        probs, alphas = [], []
        for p in range(per_group):
            here = slice(p * BLOCK, (p + 1) * BLOCK)
            q_scale = scalar_ref[2, 0, g * per_group + p]
            tiles = [
                scores[i // 2][here, (i % 2) * BLOCK : (i % 2 + 1) * BLOCK] * (q_scale * scales[i])
                for i in range(2 * len(pairs))
            ]
            top = functools.reduce(jnp.maximum, tiles)
            top = jnp.max(top, axis=1, keepdims=True)
            top = jnp.broadcast_to(top, (BLOCK, DH))
            if not first:
                old = m_ref[g, here, :]
                top = jnp.maximum(old, top)
                alpha = jnp.exp2(old - top)
                alphas.append(alpha)
            weights = [jnp.exp2(tile - top) for tile in tiles]
            total = functools.reduce(jnp.add, weights)
            if not first:
                total = l_ref[g, here, :] * alpha + total
            l_ref[g, here, :] = total
            if not last:
                m_ref[g, here, :] = top
            probs.append(jnp.concatenate([w.astype(jnp.bfloat16) for w in weights], axis=1))
        probs = jnp.concatenate(probs, axis=0)
        held = [kv_ref[half, pl.ds(base, 2), 1, :, lanes].reshape(2 * BLOCK, DH) for base in pairs]
        held = held[0] if len(held) == 1 else jnp.concatenate(held, axis=0)
        added = jnp.dot(probs, held, preferred_element_type=jnp.float32)
        for p in range(per_group):
            here = slice(p * BLOCK, (p + 1) * BLOCK)
            numer = added[here, :]
            if not first:
                numer = acc_ref[g, here, :] * alphas[p] + numer
            if last:
                total = jnp.sum(l_ref[g, here, :], axis=1, keepdims=True)
                o_ref[:, pl.ds(pl.multiple_of(g * width + p * DH, DH), DH)] = (
                    numer * (1.0 / total)
                ).astype(o_ref.dtype)
            else:
                acc_ref[g, here, :] = numer

    def out_copy(g):
        part = pl.ds(pl.multiple_of(g * width, DH), width)
        return pltpu.make_async_copy(o_ref.at[:, part], o_hbm.at[:, part], out_sem.at[g])

    def half_of(half):
        return pl.loop(half * per_half, (half + 1) * per_half)

    q_copy.wait()
    to_scalars.wait()
    for half in (0, 1):
        arrived(half, block_of(row, col, 1 - core))

        @half_of(half)
        def _(g):
            unit([block_of(row, col, 0)], g, True, False)

    @pl.loop(1, row + 1)
    def _(k):
        for half in (0, 1):
            climbed = block_of(row - k, col, core)
            arrived(half, climbed)

            @pl.when(above)
            def _():
                remote(half, climbed, UP).start()

            if half == 0:
                remote(half, climbed, ACROSS).start()
            else:

                @pl.when(k < row)
                def _():
                    remote(half, climbed, ACROSS).start()

            remote(half, climbed, CHIP).start()
            crossed = block_of(row - k + 1, 1 - col, core)
            arrived(half, crossed)
            remote(half, crossed, CHIP).start()
            arrived(half, block_of(row - k, col, 1 - core))
            arrived(half, block_of(row - k + 1, 1 - col, 1 - core))

            @half_of(half)
            def _(g):
                unit([block_of(row - k, col, 0), block_of(row - k + 1, 1 - col, 0)], g, False, False)

    crossed = block_of(0, 1 - col, core)
    for half in (0, 1):
        arrived(half, crossed)
        if half == 1:

            @pl.when(above)
            def _():
                remote(half, crossed, UP).start()

        remote(half, crossed, CHIP).start()
        arrived(half, block_of(0, 1 - col, 1 - core))

        @half_of(half)
        def _(g):
            unit([block_of(0, 1 - col, 0)], g, False, True)
            out_copy(g).start()

    @pl.loop(0, row + 1)
    def _(k):
        climbed = block_of(row - k, col, core)
        for half in (0, 1):

            @pl.when(above)
            def _():
                remote(half, climbed, UP).wait_send()

            if half == 0:
                remote(half, climbed, ACROSS).wait_send()
            else:

                @pl.when((k == 0) | (k < row))
                def _():
                    remote(half, climbed, ACROSS).wait_send()

            remote(half, climbed, CHIP).wait_send()
            remote(half, block_of(row - k, 1 - col, core), CHIP).wait_send()

    @pl.when(above)
    def _():
        remote(1, crossed, UP).wait_send()

    @pl.loop(0, groups)
    def _(g):
        out_copy(g).wait()


def attend(mesh, query_int, key_int, values, query_scale, key_scale, verticals, slashes):
    spans = mesh.shape["blk"]
    tokens = query_int.shape[0]
    blocks = key_scale.shape[0]
    heads = query_int.shape[1] // DH
    groups = key_int.shape[1] // DH
    assert tokens == BLOCK and mesh.shape["ulysses"] == 2 and spans % 2 == 0
    assert blocks == spans * 2
    assert groups % 2 == 0 and max(heads, blocks) <= 128
    per_group = heads // groups
    stack = (groups, per_group * BLOCK, DH)
    hbm = pl.BlockSpec(memory_space=pl.ANY)
    return pl.pallas_call(
        functools.partial(kernel, spans // 2, heads, groups, blocks),
        out_shape=jax.ShapeDtypeStruct(query_int.shape, jnp.bfloat16),
        in_specs=[hbm] * 7,
        out_specs=hbm,
        scratch_shapes=[
            pltpu.VMEM(query_int.shape, jnp.bfloat16),
            pltpu.VMEM((2, blocks, 2, BLOCK, groups // 2 * DH), jnp.bfloat16),
            pltpu.VMEM(stack, jnp.float32),
            pltpu.VMEM(stack, jnp.float32),
            pltpu.VMEM(stack, jnp.float32),
            pltpu.VMEM(query_int.shape, jnp.bfloat16),
            pltpu.VMEM(query_scale.shape, query_scale.dtype),
            pltpu.VMEM(key_scale.shape[::-1], key_scale.dtype),
            pltpu.VMEM(verticals.shape, jnp.int32),
            pltpu.VMEM(slashes.shape, jnp.int32),
            pltpu.VMEM((3, groups, 128), jnp.float32),
            pltpu.SMEM((3, groups, 128), jnp.float32),
            pltpu.SemaphoreType.DMA((2, 2)),
            pltpu.SemaphoreType.DMA((6,)),
            pltpu.SemaphoreType.DMA((groups,)),
            pltpu.SemaphoreType.DMA((2, 3, blocks)),
            pltpu.SemaphoreType.DMA((2, blocks)),
        ],
        compiler_params=pltpu.CompilerParams(
            collective_id=0, has_side_effects=True, vmem_limit_bytes=62 * 1024 * 1024
        ),
    )(query_int, key_int, values, query_scale, key_scale.T, verticals, slashes)


def solution(mesh):
    in_specs = (
        P(("group", "blk", "ulysses"), None),
        P(("group", "blk", "ulysses"), None),
        P(("group", "blk", "ulysses"), None),
        P(("group", "blk"), None),
        P("group", None),
        P("group", None),
        P("group", None),
    )
    out_specs = P(("group", "blk", "ulysses"), None)
    return jax.shard_map(
        functools.partial(attend, mesh),
        mesh=mesh,
        in_specs=in_specs,
        out_specs=out_specs,
        check_vma=False,
    )
```

time: 65.6 us -> 56.4 us (0.86)
  Pallas kernels: 57.8 us -> 53.1 us
  other arithmetic: 3.45 us -> 0 us
  local copies, waits for them, and re-layouts: 4.03 us -> 3.1 us
    pallas_call x1, Pallas kernels: 57.8 us -> 53.1 us  [attend(): pl.pallas_call(functools.partial(kernel, spans // 2, heads, groups, block...]
    convert_element_type x1 -> x0, other arithmetic: 1.2 us -> none  [attend(): lax.dynamic_slice_in_dim(query_scale, core, 1, 0).astype(jnp.float32)]
    reduce_or x2 -> x0, other arithmetic: 0.87 us -> none  [the longest x1 0.78 us: attend(): jnp.any(block == verticals[None], axis=2) & (block[:, :, 0] <= mine)]
    convert_element_type x1 -> x0, local copies, waits for them, and re-layouts: 0.75 us -> none  [attend(): key_scales = key_scale.astype(jnp.float32) * LOG2E]
    sub x1 -> x0, other arithmetic: 0.69 us -> none  [attend(): mine - slashes[None]]
    select_n x1 -> x0, other arithmetic: 0.68 us -> none  [attend(): bias = jnp.where(live, 0.0, -BIG).astype(jnp.float32)]
where the time goes in v2:
time: 56.4 us; the launch traced here: 56.2 us
  Pallas kernels  53.1 us (94%)
  local copies, waits for them, and re-layouts  3.1 us (5%)
    pallas_call x1, Pallas kernels, attend(): pl.pallas_call(functools.partial(kernel, spans // 2, heads, groups, block...  53.1 us
    unnamed x1, local copies, waits for them, and re-layouts  3.1 us

profile of v2, /device:TPU:25, one launch (start us, length us, event | category | flops | bytes accessed | tf_op | source)
XLA Modules:
  0.0 56.2 jit_solution(17623089821699809666)
XLA Ops:
  0.0 53.1 %shard_map.73 = bf16[128,8192]{1,0:T(8,128)(2,1)} custom-call(bf16[128,8192]{1,0:T(8,128)(2,1)} %q_hbm.1, bf16[128,1024]{1,0:T(8,128)(2,1)} %k_hbm.1, bf16[128,1024]{1,0:T(8,128)(2,1)} %v_hbm.1, bf16[2,64]{1,0:T(2,128)(2,1)} %qs_hbm.1, bf16[8,16]{1,0:T(8,128)(2,1)} %bitcast.1, s32[8,8]{1,0:T(8,128)} %vert_hbm.1, s32[8,8]{1,0:T(8,128)} %slash_hbm.1), custom_call_target="tpu_custom_call" | custom-call | tf_op jit(solution)/shard_map/pallas_call | solution.py:302
  53.1 3.1 %copy.9 = bf16[128,8192]{1,0:T(8,128)(2,1)} copy(bf16[128,8192]{1,0:T(8,128)(2,1)} %shard_map.73) | data formatting | bytes 4194304

commit v3 on v2

--- a/solution.py
+++ b/solution.py
@@ -27,8 +27,9 @@
     mine = span * 2 + core
     per_group = heads // groups
     width = per_group * DH
-    per_half = groups // 2
-    half_lanes = per_half * DH
+    parts = kv_ref.shape[0]
+    per_part = groups // parts
+    part_lanes = per_part * DH
 
     def block_of(r, c, u):
         return (r * 2 + c) * 2 + u
@@ -40,25 +41,25 @@
             return {"blk": row * 2 + 1 - col, "ulysses": core}
         return {"blk": span, "ulysses": 1 - core}
 
-    def remote(half, block, way):
-        place = kv_ref.at[half, block]
+    def remote(part, block, way):
+        place = kv_ref.at[part, block]
         return pltpu.make_async_remote_copy(
             src_ref=place,
             dst_ref=place,
-            send_sem=send_sem.at[half, way, block],
-            recv_sem=recv_sem.at[half, block],
+            send_sem=send_sem.at[part, way, block],
+            recv_sem=recv_sem.at[part, block],
             device_id=target(way),
             device_id_type=MESH,
         )
 
-    def arrived(half, block):
-        remote(half, block, CHIP).wait_recv()
-
-    def local_copy(half, which):
+    def arrived(part, block):
+        remote(part, block, CHIP).wait_recv()
+
+    def local_copy(part, which):
         return pltpu.make_async_copy(
-            (k_hbm, v_hbm)[which].at[:, pl.ds(half * half_lanes, half_lanes)],
-            kv_ref.at[half, mine, which],
-            local_sem.at[half, which],
+            (k_hbm, v_hbm)[which].at[:, pl.ds(part * part_lanes, part_lanes)],
+            kv_ref.at[part, mine, which],
+            local_sem.at[part, which],
         )
 
     small = [
@@ -69,9 +70,9 @@
     ]
     to_scalars = pltpu.make_async_copy(table_ref, scalar_ref, small_sem.at[4])
     q_copy = pltpu.make_async_copy(q_hbm, q_ref, small_sem.at[5])
-    for half in (0, 1):
+    for part in range(parts):
         for which in (0, 1):
-            local_copy(half, which).start()
+            local_copy(part, which).start()
     for copy in small:
         copy.start()
     q_copy.start()
@@ -95,16 +96,16 @@
         pl.semaphore_signal(barrier, inc=1, device_id=target(way), device_id_type=MESH)
     pl.semaphore_wait(barrier, 2 + below.astype(jnp.int32) + above.astype(jnp.int32))
 
-    for half in (0, 1):
+    for part in range(parts):
         for which in (0, 1):
-            local_copy(half, which).wait()
+            local_copy(part, which).wait()
 
         @pl.when(above)
         def _():
-            remote(half, mine, UP).start()
-
-        remote(half, mine, ACROSS).start()
-        remote(half, mine, CHIP).start()
+            remote(part, mine, UP).start()
+
+        remote(part, mine, ACROSS).start()
+        remote(part, mine, CHIP).start()
 
     for copy in small:
         copy.wait()
@@ -130,9 +131,9 @@
         own = jnp.where(block == mine, -BIG, 0.0)
         return (scalar_ref[0, g, block] + later * own).astype(jnp.bfloat16)
 
-    def unit(pairs, g, first, last):
-        half = g // per_half
-        lanes = pl.ds(pl.multiple_of((g - half * per_half) * DH, DH), DH)
+    def unit(pairs, part, i, first, last):
+        g = part * per_part + i
+        lanes = slice(i * DH, (i + 1) * DH)
         queries = jnp.concatenate(
             [
                 jnp.concatenate(
@@ -144,7 +145,7 @@
         )
         scores, scales = [], []
         for base in pairs:
-            keys = kv_ref[half, pl.ds(base, 2), 0, :, lanes].reshape(2 * BLOCK, DH)
+            keys = kv_ref[part, pl.ds(base, 2), 0, :, lanes].reshape(2 * BLOCK, DH)
             mask = jnp.concatenate([hidden(base, g), hidden(base + 1, g)], axis=0)
             scores.append(
                 lax.dot_general(
@@ -180,7 +181,7 @@
                 m_ref[g, here, :] = top
             probs.append(jnp.concatenate([w.astype(jnp.bfloat16) for w in weights], axis=1))
         probs = jnp.concatenate(probs, axis=0)
-        held = [kv_ref[half, pl.ds(base, 2), 1, :, lanes].reshape(2 * BLOCK, DH) for base in pairs]
+        held = [kv_ref[part, pl.ds(base, 2), 1, :, lanes].reshape(2 * BLOCK, DH) for base in pairs]
         held = held[0] if len(held) == 1 else jnp.concatenate(held, axis=0)
         added = jnp.dot(probs, held, preferred_element_type=jnp.float32)
         for p in range(per_group):
@@ -200,87 +201,82 @@
         part = pl.ds(pl.multiple_of(g * width, DH), width)
         return pltpu.make_async_copy(o_ref.at[:, part], o_hbm.at[:, part], out_sem.at[g])
 
-    def half_of(half):
-        return pl.loop(half * per_half, (half + 1) * per_half)
-
     q_copy.wait()
     to_scalars.wait()
-    for half in (0, 1):
-        arrived(half, block_of(row, col, 1 - core))
-
-        @half_of(half)
-        def _(g):
-            unit([block_of(row, col, 0)], g, True, False)
+
+    @pl.loop(0, parts)
+    def _(part):
+        arrived(part, block_of(row, col, 1 - core))
+        for i in range(per_part):
+            unit([block_of(row, col, 0)], part, i, True, False)
+
+    def crosses(part, k):
+        return (part < parts // 2) | (k < row)
 
     @pl.loop(1, row + 1)
     def _(k):
-        for half in (0, 1):
+        @pl.loop(0, parts)
+        def _(part):
             climbed = block_of(row - k, col, core)
-            arrived(half, climbed)
+            arrived(part, climbed)
 
             @pl.when(above)
             def _():
-                remote(half, climbed, UP).start()
-
-            if half == 0:
-                remote(half, climbed, ACROSS).start()
-            else:
-
-                @pl.when(k < row)
-                def _():
-                    remote(half, climbed, ACROSS).start()
-
-            remote(half, climbed, CHIP).start()
+                remote(part, climbed, UP).start()
+
+            @pl.when(crosses(part, k))
+            def _():
+                remote(part, climbed, ACROSS).start()
+
+            remote(part, climbed, CHIP).start()
             crossed = block_of(row - k + 1, 1 - col, core)
-            arrived(half, crossed)
-            remote(half, crossed, CHIP).start()
-            arrived(half, block_of(row - k, col, 1 - core))
-            arrived(half, block_of(row - k + 1, 1 - col, 1 - core))
-
-            @half_of(half)
-            def _(g):
-                unit([block_of(row - k, col, 0), block_of(row - k + 1, 1 - col, 0)], g, False, False)
+            arrived(part, crossed)
+            remote(part, crossed, CHIP).start()
+            arrived(part, block_of(row - k, col, 1 - core))
+            arrived(part, block_of(row - k + 1, 1 - col, 1 - core))
+            bases = [block_of(row - k, col, 0), block_of(row - k + 1, 1 - col, 0)]
+            for i in range(per_part):
+                unit(bases, part, i, False, False)
 
     crossed = block_of(0, 1 - col, core)
-    for half in (0, 1):
-        arrived(half, crossed)
-        if half == 1:
-
-            @pl.when(above)
-            def _():
-                remote(half, crossed, UP).start()
-
-        remote(half, crossed, CHIP).start()
-        arrived(half, block_of(0, 1 - col, 1 - core))
-
-        @half_of(half)
-        def _(g):
-            unit([block_of(0, 1 - col, 0)], g, False, True)
-            out_copy(g).start()
+
+    @pl.loop(0, parts)
+    def _(step):
+        part = step % 2 * (parts // 2) + step // 2
+        arrived(part, crossed)
+
+        @pl.when(above & (part >= parts // 2))
+        def _():
+            remote(part, crossed, UP).start()
+
+        remote(part, crossed, CHIP).start()
+        arrived(part, block_of(0, 1 - col, 1 - core))
+        for i in range(per_part):
+            unit([block_of(0, 1 - col, 0)], part, i, False, True)
+            out_copy(part * per_part + i).start()
 
     @pl.loop(0, row + 1)
     def _(k):
         climbed = block_of(row - k, col, core)
-        for half in (0, 1):
-
+
+        @pl.loop(0, parts)
+        def _(part):
             @pl.when(above)
             def _():
-                remote(half, climbed, UP).wait_send()
-
-            if half == 0:
-                remote(half, climbed, ACROSS).wait_send()
-            else:
-
-                @pl.when((k == 0) | (k < row))
-                def _():
-                    remote(half, climbed, ACROSS).wait_send()
-
-            remote(half, climbed, CHIP).wait_send()
-            remote(half, block_of(row - k, 1 - col, core), CHIP).wait_send()
+                remote(part, climbed, UP).wait_send()
+
+            @pl.when((k == 0) | crosses(part, k))
+            def _():
+                remote(part, climbed, ACROSS).wait_send()
+
+            remote(part, climbed, CHIP).wait_send()
+            remote(part, block_of(row - k, 1 - col, core), CHIP).wait_send()
 
     @pl.when(above)
     def _():
-        remote(1, crossed, UP).wait_send()
+        @pl.loop(parts // 2, parts)
+        def _(part):
+            remote(part, crossed, UP).wait_send()
 
     @pl.loop(0, groups)
     def _(g):
@@ -295,7 +291,8 @@
     groups = key_int.shape[1] // DH
     assert tokens == BLOCK and mesh.shape["ulysses"] == 2 and spans % 2 == 0
     assert blocks == spans * 2
-    assert groups % 2 == 0 and max(heads, blocks) <= 128
+    parts = 4
+    assert groups % parts == 0 and max(heads, blocks) <= 128
     per_group = heads // groups
     stack = (groups, per_group * BLOCK, DH)
     hbm = pl.BlockSpec(memory_space=pl.ANY)
@@ -306,7 +303,7 @@
         out_specs=hbm,
         scratch_shapes=[
             pltpu.VMEM(query_int.shape, jnp.bfloat16),
-            pltpu.VMEM((2, blocks, 2, BLOCK, groups // 2 * DH), jnp.bfloat16),
+            pltpu.VMEM((parts, blocks, 2, BLOCK, groups // parts * DH), jnp.bfloat16),
             pltpu.VMEM(stack, jnp.float32),
             pltpu.VMEM(stack, jnp.float32),
             pltpu.VMEM(stack, jnp.float32),
@@ -317,11 +314,11 @@
             pltpu.VMEM(slashes.shape, jnp.int32),
             pltpu.VMEM((3, groups, 128), jnp.float32),
             pltpu.SMEM((3, groups, 128), jnp.float32),
-            pltpu.SemaphoreType.DMA((2, 2)),
+            pltpu.SemaphoreType.DMA((parts, 2)),
             pltpu.SemaphoreType.DMA((6,)),
             pltpu.SemaphoreType.DMA((groups,)),
-            pltpu.SemaphoreType.DMA((2, 3, blocks)),
-            pltpu.SemaphoreType.DMA((2, blocks)),
+            pltpu.SemaphoreType.DMA((parts, 3, blocks)),
+            pltpu.SemaphoreType.DMA((parts, blocks)),
         ],
         compiler_params=pltpu.CompilerParams(
             collective_id=0, has_side_effects=True, vmem_limit_bytes=62 * 1024 * 1024

time: 56.4 us -> 58.5 us (1.037)
  Pallas kernels: 53.1 us -> 55.2 us
    pallas_call x1, Pallas kernels: 53.1 us -> 55.2 us  [attend(): pl.pallas_call(functools.partial(kernel, spans // 2, heads, groups, block...]
where the time goes in v3:
time: 58.5 us; the launch traced here: 58.3 us
  Pallas kernels  55.2 us (94%)
  local copies, waits for them, and re-layouts  3.1 us (5%)
    pallas_call x1, Pallas kernels, attend(): pl.pallas_call(functools.partial(kernel, spans // 2, heads, groups, block...  55.2 us
    unnamed x1, local copies, waits for them, and re-layouts  3.1 us

profile of v3, /device:TPU:25, one launch (start us, length us, event | category | flops | bytes accessed | tf_op | source)
XLA Modules:
  0.0 58.3 jit_solution(10084736232614156485)
XLA Ops:
  0.0 55.2 %shard_map.73 = bf16[128,8192]{1,0:T(8,128)(2,1)} custom-call(bf16[128,8192]{1,0:T(8,128)(2,1)} %q_hbm.1, bf16[128,1024]{1,0:T(8,128)(2,1)} %k_hbm.1, bf16[128,1024]{1,0:T(8,128)(2,1)} %v_hbm.1, bf16[2,64]{1,0:T(2,128)(2,1)} %qs_hbm.1, bf16[8,16]{1,0:T(8,128)(2,1)} %bitcast.1, s32[8,8]{1,0:T(8,128)} %vert_hbm.1, s32[8,8]{1,0:T(8,128)} %slash_hbm.1), custom_call_target="tpu_custom_call" | custom-call | tf_op jit(solution)/shard_map/pallas_call | solution.py:299
  55.2 3.1 %copy.9 = bf16[128,8192]{1,0:T(8,128)(2,1)} copy(bf16[128,8192]{1,0:T(8,128)(2,1)} %shard_map.73) | data formatting | bytes 4194304

commit v4 on v3

--- a/solution.py
+++ b/solution.py
@@ -213,43 +213,70 @@
     def crosses(part, k):
         return (part < parts // 2) | (k < row)
 
-    @pl.loop(1, row + 1)
-    def _(k):
-        @pl.loop(0, parts)
-        def _(part):
-            climbed = block_of(row - k, col, core)
-            arrived(part, climbed)
-
-            @pl.when(above)
-            def _():
-                remote(part, climbed, UP).start()
-
-            @pl.when(crosses(part, k))
-            def _():
-                remote(part, climbed, ACROSS).start()
-
-            remote(part, climbed, CHIP).start()
-            crossed = block_of(row - k + 1, 1 - col, core)
-            arrived(part, crossed)
-            remote(part, crossed, CHIP).start()
+    def pass_on(k, part):
+        climbed = block_of(row - k, col, core)
+        arrived(part, climbed)
+
+        @pl.when(above)
+        def _():
+            remote(part, climbed, UP).start()
+
+        @pl.when(crosses(part, k))
+        def _():
+            remote(part, climbed, ACROSS).start()
+
+        remote(part, climbed, CHIP).start()
+        crossed = block_of(row - k + 1, 1 - col, core)
+        arrived(part, crossed)
+        remote(part, crossed, CHIP).start()
+
+    crossed = block_of(0, 1 - col, core)
+
+    def pass_last_on(part):
+        arrived(part, crossed)
+
+        @pl.when(above & (part >= parts // 2))
+        def _():
+            remote(part, crossed, UP).start()
+
+        remote(part, crossed, CHIP).start()
+
+    def last_part(step):
+        return step % 2 * (parts // 2) + step // 2
+
+    turns = row * parts
+
+    @pl.loop(0, turns + 1)
+    def _(turn):
+        @pl.when(turn < turns)
+        def _():
+            pass_on(1 + turn // parts, turn % parts)
+
+        @pl.when(turn == turns)
+        def _():
+            pass_last_on(last_part(0))
+
+        @pl.when(turn > 0)
+        def _():
+            k, part = 1 + (turn - 1) // parts, (turn - 1) % parts
             arrived(part, block_of(row - k, col, 1 - core))
             arrived(part, block_of(row - k + 1, 1 - col, 1 - core))
             bases = [block_of(row - k, col, 0), block_of(row - k + 1, 1 - col, 0)]
             for i in range(per_part):
                 unit(bases, part, i, False, False)
 
-    crossed = block_of(0, 1 - col, core)
-
     @pl.loop(0, parts)
     def _(step):
-        part = step % 2 * (parts // 2) + step // 2
-        arrived(part, crossed)
-
-        @pl.when(above & (part >= parts // 2))
-        def _():
-            remote(part, crossed, UP).start()
-
-        remote(part, crossed, CHIP).start()
+        part = last_part(step)
+
+        @pl.when(step % 2 == 0)
+        def _():
+            @pl.when(step > 0)
+            def _():
+                pass_last_on(part)
+
+            pass_last_on(last_part(step + 1))
+
         arrived(part, block_of(0, 1 - col, 1 - core))
         for i in range(per_part):
             unit([block_of(0, 1 - col, 0)], part, i, False, True)

time: 58.5 us -> 54.9 us (0.938)
  Pallas kernels: 55.2 us -> 51.7 us
    pallas_call x1, Pallas kernels: 55.2 us -> 51.7 us  [attend(): pl.pallas_call(functools.partial(kernel, spans // 2, heads, groups, block...]
where the time goes in v4:
time: 54.9 us; the launch traced here: 54.8 us
  Pallas kernels  51.7 us (94%)
  local copies, waits for them, and re-layouts  3.1 us (6%)
    pallas_call x1, Pallas kernels, attend(): pl.pallas_call(functools.partial(kernel, spans // 2, heads, groups, block...  51.7 us
    unnamed x1, local copies, waits for them, and re-layouts  3.1 us

profile of v4, /device:TPU:25, one launch (start us, length us, event | category | flops | bytes accessed | tf_op | source)
XLA Modules:
  0.0 54.8 jit_solution(8104145935422788198)
XLA Ops:
  0.0 51.7 %shard_map.73 = bf16[128,8192]{1,0:T(8,128)(2,1)} custom-call(bf16[128,8192]{1,0:T(8,128)(2,1)} %q_hbm.1, bf16[128,1024]{1,0:T(8,128)(2,1)} %k_hbm.1, bf16[128,1024]{1,0:T(8,128)(2,1)} %v_hbm.1, bf16[2,64]{1,0:T(2,128)(2,1)} %qs_hbm.1, bf16[8,16]{1,0:T(8,128)(2,1)} %bitcast.1, s32[8,8]{1,0:T(8,128)} %vert_hbm.1, s32[8,8]{1,0:T(8,128)} %slash_hbm.1), custom_call_target="tpu_custom_call" | custom-call | tf_op jit(solution)/shard_map/pallas_call | solution.py:326
  51.7 3.1 %copy.9 = bf16[128,8192]{1,0:T(8,128)(2,1)} copy(bf16[128,8192]{1,0:T(8,128)(2,1)} %shard_map.73) | data formatting | bytes 4194304

commit v5 on v4

--- a/solution.py
+++ b/solution.py
@@ -17,9 +17,9 @@
 
 
 def kernel(
-    rows, heads, groups, blocks, q_hbm, k_hbm, v_hbm, qs_hbm, ks_hbm, vert_hbm, slash_hbm, o_hbm,
-    q_ref, kv_ref, m_ref, l_ref, acc_ref, o_ref, qs_ref, ks_ref, vert_ref, slash_ref,
-    table_ref, scalar_ref, local_sem, small_sem, out_sem, send_sem, recv_sem,
+    rows, heads, groups, blocks, q_hbm, k_hbm, v_hbm, qs_hbm, ks_hbm, vert_hbm, slash_hbm, o_ref,
+    q_ref, kv_ref, m_ref, l_ref, acc_ref, qs_ref, ks_ref, vert_ref, slash_ref,
+    table_ref, scalar_ref, local_sem, small_sem, send_sem, recv_sem,
 ):
     span = lax.axis_index("blk")
     core = lax.axis_index("ulysses")
@@ -197,10 +197,6 @@
             else:
                 acc_ref[g, here, :] = numer
 
-    def out_copy(g):
-        part = pl.ds(pl.multiple_of(g * width, DH), width)
-        return pltpu.make_async_copy(o_ref.at[:, part], o_hbm.at[:, part], out_sem.at[g])
-
     q_copy.wait()
     to_scalars.wait()
 
@@ -280,7 +276,6 @@
         arrived(part, block_of(0, 1 - col, 1 - core))
         for i in range(per_part):
             unit([block_of(0, 1 - col, 0)], part, i, False, True)
-            out_copy(part * per_part + i).start()
 
     @pl.loop(0, row + 1)
     def _(k):
@@ -304,10 +299,6 @@
         @pl.loop(parts // 2, parts)
         def _(part):
             remote(part, crossed, UP).wait_send()
-
-    @pl.loop(0, groups)
-    def _(g):
-        out_copy(g).wait()
 
 
 def attend(mesh, query_int, key_int, values, query_scale, key_scale, verticals, slashes):
@@ -327,14 +318,13 @@
         functools.partial(kernel, spans // 2, heads, groups, blocks),
         out_shape=jax.ShapeDtypeStruct(query_int.shape, jnp.bfloat16),
         in_specs=[hbm] * 7,
-        out_specs=hbm,
+        out_specs=pl.BlockSpec(memory_space=pltpu.VMEM),
         scratch_shapes=[
             pltpu.VMEM(query_int.shape, jnp.bfloat16),
             pltpu.VMEM((parts, blocks, 2, BLOCK, groups // parts * DH), jnp.bfloat16),
             pltpu.VMEM(stack, jnp.float32),
             pltpu.VMEM(stack, jnp.float32),
             pltpu.VMEM(stack, jnp.float32),
-            pltpu.VMEM(query_int.shape, jnp.bfloat16),
             pltpu.VMEM(query_scale.shape, query_scale.dtype),
             pltpu.VMEM(key_scale.shape[::-1], key_scale.dtype),
             pltpu.VMEM(verticals.shape, jnp.int32),
@@ -343,14 +333,13 @@
             pltpu.SMEM((3, groups, 128), jnp.float32),
             pltpu.SemaphoreType.DMA((parts, 2)),
             pltpu.SemaphoreType.DMA((6,)),
-            pltpu.SemaphoreType.DMA((groups,)),
             pltpu.SemaphoreType.DMA((parts, 3, blocks)),
             pltpu.SemaphoreType.DMA((parts, blocks)),
         ],
         compiler_params=pltpu.CompilerParams(
-            collective_id=0, has_side_effects=True, vmem_limit_bytes=62 * 1024 * 1024
+            collective_id=0, has_side_effects=True, vmem_limit_bytes=(20 + blocks // 2) * 1024 * 1024
         ),
-    )(query_int, key_int, values, query_scale, key_scale.T, verticals, slashes)
+    )(*[pltpu.with_memory_space_constraint(x, pltpu.HBM) for x in (query_int, key_int, values, query_scale, key_scale.T, verticals, slashes)])
 
 
 def solution(mesh):

time: 54.9 us -> 52.7 us (0.960)
  local copies, waits for them, and re-layouts: 3.1 us -> 1.32 us
    unnamed x1, local copies, waits for them, and re-layouts: 3.1 us -> 1.32 us
where the time goes in v5:
time: 52.7 us; the launch traced here: 52.5 us
  Pallas kernels  51.2 us (97%)
  local copies, waits for them, and re-layouts  1.32 us (3%)
    pallas_call x1, Pallas kernels, attend(): pl.pallas_call(functools.partial(kernel, spans // 2, heads, groups, block...  51.2 us
    unnamed x1, local copies, waits for them, and re-layouts  1.32 us

profile of v5, /device:TPU:25, one launch (start us, length us, event | category | flops | bytes accessed | tf_op | source)
XLA Modules:
  0.0 52.5 jit_solution(8821126941733901836)
XLA Ops:
  0.0 51.2 %shard_map.73 = bf16[128,8192]{1,0:T(8,128)(2,1)S(1)} custom-call(bf16[128,8192]{1,0:T(8,128)(2,1)} %q_hbm.1, bf16[128,1024]{1,0:T(8,128)(2,1)} %k_hbm.1, bf16[128,1024]{1,0:T(8,128)(2,1)} %v_hbm.1, bf16[2,64]{1,0:T(2,128)(2,1)} %qs_hbm.1, bf16[8,16]{1,0:T(8,128)(2,1)} %bitcast.1, s32[8,8]{1,0:T(8,128)} %vert_hbm.1, s32[8,8]{1,0:T(8,128)} %slash_hbm.1), custom_call_target="tpu_custom_call" | custom-call | tf_op jit(solution)/shard_map/pallas_call | solution.py:317
  51.2 1.3 %copy.9 = bf16[128,8192]{1,0:T(8,128)(2,1)} copy(bf16[128,8192]{1,0:T(8,128)(2,1)S(1)} %shard_map.73) | data formatting | bytes 4194304
